TPU v7x, 512 devices: a whole 4x4x16 slice. The times are simulated.
512 devices in a mesh: section: 2 (over x_hi), expert: 32 (over z, core), tensor: 8 (over x_lo, y).
Axes of the slice: x: 4 (x_hi: 2, x_lo: 2; x = x_hi * 2 + x_lo), y: 4, z: 16, core: 2. Of those that a mesh axis runs over, the one named last changes fastest.
Arguments:
- tokens: bfloat16 [8192, 2880], P(('section', 'expert'), 'tensor'), may hold values from -6 to 6
- expert_ids: int32 [8192, 4], P(('section', 'expert')), may hold values from 0 to 63, as said below
- gates: float32 [8192, 4], P(('section', 'expert')), may hold values from 0.05 to 0.5
- remap: int32 [64], replicated, may hold values from 0 to 63, as said below
- gate_up: bfloat16 [64, 2, 1440, 2880], P(('section', 'expert'), None, 'tensor'), may hold values from -0.109375 to 0.109375
- down: bfloat16 [64, 1440, 2880], P(('section', 'expert'), None, 'tensor'), may hold values from -0.15625 to 0.15625
- norm_gain: float32 [2880], replicated, may hold values from 0.25 to 1.75
- w_query: bfloat16 [2880, 2048], P(('section', 'expert'), 'tensor'), may hold values from -2 to 2
- w_key: bfloat16 [2880, 512], P(('section', 'expert'), 'tensor'), may hold values from -2 to 2
- w_value: bfloat16 [2880, 512], P(('section', 'expert'), 'tensor'), may hold values from -0.109375 to 0.109375
- w_out: bfloat16 [2048, 2880], P('tensor', ('section', 'expert')), may hold values from -0.125 to 0.125
Outputs:
- stream: bfloat16 [8192, 2880], P(('section', 'expert'), 'tensor')
- attended: bfloat16 [8192, 2880], P(('section', 'expert'), 'tensor')
Inputs may be any that keep to these rules, and one draw needn't show every extreme that they name: `remap`: every expert maps to itself, except the 4 experts of one aligned group of 4 (a failed host), which map to 4 different surviving experts. `expert_ids`: each row names 4 different experts, and their images under remap differ too. In every aligned block of 128 rows, after the remap, 4 surviving experts receive exactly 16 picks each, every other surviving expert exactly 8, the experts of the failed host none.
All inputs are finite; a program needn't handle non-finite values.
Results may differ from a plain program's by a relative error of at most 0.033.
Values may be sent and summed in bfloat16 or wider, within the bound.
No kernel may reach another device: no remote copies, remote signals or barrier semaphores. Data moves between devices by JAX's collectives and lax.ppermute only.
A program may use at most 64 MiB of HBM per device.

v0:
```python
import math
import jax
import jax.numpy as jnp
from jax import lax
from jax.sharding import PartitionSpec as P

D = 2880
HD = 64
epsilon = 1e-05


def rotate_pairs(values, positions):
    half_size = values.shape[-1] // 2
    freq = jnp.exp(
        -math.log(150000.0) * jnp.arange(half_size, dtype=jnp.float32) * 2.0 / values.shape[-1]
    )
    angle = positions.astype(jnp.float32)[:, None] * freq[None, :]
    cosine = jnp.cos(angle)[:, None, :]
    sine = jnp.sin(angle)[:, None, :]
    first_half = values[..., :half_size]
    second_half = values[..., half_size:]
    return jnp.concatenate(
        [first_half * cosine - second_half * sine, second_half * cosine + first_half * sine],
        axis=-1,
    )


def on_device(
    tokens, expert_ids, gates, remap, gate_up, down, norm_gain, w_query, w_key, w_value, w_out
):
    token_rows = tokens.shape[0]
    slice_width = tokens.shape[1]
    topk_count = expert_ids.shape[1]
    groups = lax.axis_size(("section", "expert"))
    capacity = 2 * token_rows * topk_count // groups
    physical = remap[expert_ids].reshape(-1)
    pick_count = physical.shape[0]
    pick_token = jnp.arange(pick_count, dtype=jnp.int32) // topk_count
    one_hot = (physical[:, None] == jnp.arange(groups, dtype=jnp.int32)[None, :]).astype(jnp.int32)
    pick_rank = jnp.sum((jnp.cumsum(one_hot, axis=0) - 1) * one_hot, axis=1)
    slot_index = physical * capacity + pick_rank
    slot_hits = slot_index[:, None] == jnp.arange(groups * capacity, dtype=jnp.int32)[None, :]
    slot_token = jnp.sum(jnp.where(slot_hits, pick_token[:, None], 0), axis=0)
    slot_used = jnp.any(slot_hits, axis=0)
    local_hidden = gate_up.shape[2]
    local_expert = gate_up[0].reshape(2 * local_hidden, gate_up.shape[3])
    whole_tokens = lax.all_gather(tokens, "tensor", axis=1, tiled=True)
    outgoing = jnp.where(
        slot_used[:, None], whole_tokens[slot_token], jnp.zeros((), jnp.bfloat16)
    ).reshape(groups, capacity, -1)
    arrived = lax.all_to_all(
        outgoing, ("section", "expert"), split_axis=0, concat_axis=0, tiled=True
    )
    source_count = arrived.shape[0]
    rows_in = arrived.reshape(-1, arrived.shape[2])
    projected = lax.dot_general(
        rows_in, local_expert, (((1,), (1,)), ((), ())), preferred_element_type=jnp.float32
    )
    hidden = (jax.nn.silu(projected[:, :local_hidden]) * projected[:, local_hidden:]).astype(
        jnp.bfloat16
    )
    all_hidden = lax.all_gather(hidden, "tensor", axis=1, tiled=True)
    result = jnp.dot(all_hidden, down[0], preferred_element_type=jnp.float32).astype(jnp.bfloat16)
    result = result.reshape(source_count, -1, result.shape[1])
    returned = lax.all_to_all(
        result, ("section", "expert"), split_axis=0, concat_axis=0, tiled=True
    )
    back_rows = returned.reshape(groups * capacity, -1)[slot_index]
    mixture = jnp.sum(
        back_rows.astype(jnp.float32).reshape(token_rows, topk_count, -1) * gates[:, :, None],
        axis=1,
    )
    stream = (tokens.astype(jnp.float32) + mixture).astype(jnp.bfloat16)
    stream_wide = stream.astype(jnp.float32)
    squares = lax.psum(jnp.sum(stream_wide * stream_wide, axis=1), "tensor")
    gain_part = lax.dynamic_slice_in_dim(
        norm_gain, lax.axis_index("tensor") * slice_width, slice_width
    )
    normed_part = (
        stream_wide * lax.rsqrt(squares / D + epsilon)[:, None] * gain_part[None, :]
    ).astype(jnp.bfloat16)
    normed = lax.all_gather(normed_part, "tensor", axis=1, tiled=True)
    query_width = w_query.shape[1]
    kv_width = w_key.shape[1]
    pieces = (
        lax.all_gather(w_query, ("section", "expert"), axis=0, tiled=True),
        lax.all_gather(w_key, ("section", "expert"), axis=0, tiled=True),
        lax.all_gather(w_value, ("section", "expert"), axis=0, tiled=True),
    )
    query_raw, key_raw, value_raw = tuple(
        (jnp.dot(normed, piece, preferred_element_type=jnp.float32) for piece in pieces)
    )
    positions = lax.axis_index("expert") * token_rows + jnp.arange(token_rows, dtype=jnp.int32)
    query_heads = query_width // HD
    kv_heads = kv_width // HD
    group_size = query_heads // kv_heads
    queries = rotate_pairs(query_raw.reshape(token_rows, query_heads, HD), positions).astype(
        jnp.bfloat16
    )
    keys = (
        rotate_pairs(key_raw.reshape(token_rows, kv_heads, HD), positions)
        .astype(jnp.bfloat16)
        .reshape(token_rows, kv_width)
    )
    values = value_raw.astype(jnp.bfloat16)
    grouped = queries.reshape(token_rows, kv_heads, group_size, HD)
    pieces = (
        lax.all_gather(keys, "expert", axis=0, tiled=True),
        lax.all_gather(values, "expert", axis=0, tiled=True),
    )
    running_max = jnp.full((kv_heads, group_size, token_rows), -1e30, jnp.float32)
    key_piece = pieces[0].reshape(-1, kv_heads, HD)
    value_piece = pieces[1].reshape(-1, kv_heads, HD)
    key_count = key_piece.shape[0]
    scores = jnp.einsum(
        "tkgd,nkd->kgtn", grouped, key_piece, preferred_element_type=jnp.float32
    ) / math.sqrt(HD)
    key_positions = jnp.arange(key_count, dtype=jnp.int32)
    allowed = key_positions[None, :] <= positions[:, None]
    scores = jnp.where(allowed, scores, -1e30)
    new_max = jnp.maximum(running_max, jnp.max(scores, axis=-1))
    weights = jnp.where(allowed, jnp.exp(scores - new_max[..., None]), 0.0)
    new_sum = jnp.sum(weights, axis=-1)
    weights_low = weights.astype(jnp.bfloat16)
    new_acc = jnp.einsum(
        "kgtn,nkd->kgtd", weights_low, value_piece, preferred_element_type=jnp.float32
    )
    heads = (
        (new_acc / new_sum[..., None])
        .transpose(2, 0, 1, 3)
        .reshape(token_rows, query_width)
        .astype(jnp.bfloat16)
    )
    partial_out = jnp.dot(
        heads,
        lax.all_gather(w_out, ("section", "expert"), axis=1, tiled=True),
        preferred_element_type=jnp.float32,
    )
    attended = lax.psum_scatter(
        partial_out.astype(jnp.bfloat16), "tensor", scatter_dimension=1, tiled=True
    )
    return (stream, attended)


def solution(mesh):
    return jax.shard_map(
        on_device,
        mesh=mesh,
        in_specs=(
            P(("section", "expert"), "tensor"),
            P(("section", "expert"), None),
            P(("section", "expert"), None),
            P(),
            P(("section", "expert"), None, "tensor", None),
            P(("section", "expert"), None, "tensor"),
            P(),
            P(("section", "expert"), "tensor"),
            P(("section", "expert"), "tensor"),
            P(("section", "expert"), "tensor"),
            P("tensor", ("section", "expert")),
        ),
        out_specs=(P(("section", "expert"), "tensor"), P(("section", "expert"), "tensor")),
        check_vma=False,
    )
```

profile of v0, /device:TPU:32, one launch (start us, length us, event | category | flops | bytes accessed | tf_op | source)
XLA Modules:
  0.0 853.0 jit_solution(9896610226944616474)
XLA Ops:
  7.2 0.8 compare_select_fusion.2
  8.2 3.3 gather_fusion
  11.6 1.2 reduce-window.6
  13.2 0.4 fusion.7
  13.9 30.1 %all_gather.27 = bf16[128,2880]{0,1:T(8,128)(2,1)S(1)} all-gather(bf16[128,360]{0,1:T(8,128)(2,1)S(1)} %copy-done.5), channel_id=1, replica_groups=mesh['section'=2,'expert'=32,'tensor'=8] {'tensor'}, dimensions={1}, use_global_device_ids=true | all-gather | bytes 829440 | tf_op jit(solution)/shard_map/all_gather | solution.py:47
  44.0 0.4 copy.57
  44.5 6.6 gather_fusion.1
  51.1 5.9 broadcast_select_fusion
  57.0 18.1 %all-to-all-start = ((bf16[64,16,2880]{2,1,0:T(8,128)(2,1)}), bf16[64,16,2880]{2,1,0:T(8,128)(2,1)}, u32[]{:S(2)}, u32[]{:S(2)}) async-start(bf16[64,16,2880]{2,1,0:T(8,128)(2,1)} %broadcast_select_fusion), calls=%async_computation | async-start | bytes 12058624 | tf_op jit(solution)/shard_map/all_to_all | solution.py:51
  75.1 1.8 copy.58
  76.9 2.3 reshape_squeeze.3
  79.3 257.8 %all-to-all-done = bf16[64,16,2880]{2,1,0:T(8,128)(2,1)} async-done(((bf16[64,16,2880]{2,1,0:T(8,128)(2,1)}), bf16[64,16,2880]{2,1,0:T(8,128)(2,1)}, u32[]{:S(2)}, u32[]{:S(2)}) %all-to-all-start) | async-done | bytes 5898272 | tf_op jit(solution)/shard_map/all_to_all | solution.py:51
  337.1 5.8 fusion.47
  343.0 1.0 fusion.19
  344.0 0.7 all-gather.11.cloned.1.call-update
  344.8 0.7 all-gather.13.cloned.1.call-update
  345.5 47.8 %all-gather.9.cloned.1.call-done = bf16[8,180,1024]{2,1,0:T(8,128)(2,1)} async-done(((bf16[1,180,1024]{2,1,0:T(8,128)(2,1)}), bf16[8,180,1024]{2,1,0:T(8,128)(2,1)}) %all-gather.9.cloned.1.call-update) | async-done | bytes 2949136 | tf_op jit(solution)/shard_map/all_gather | solution.py:62
  393.2 4.3 reshape.315
  397.6 3.2 convolution_convert_fusion.1
  400.8 1.2 copy.59
  402.0 15.3 %all-to-all-start.1 = ((bf16[64,16,360]{2,1,0:T(8,128)(2,1)}), bf16[64,16,360]{2,1,0:T(8,128)(2,1)S(1)}, u32[]{:S(2)}, u32[]{:S(2)}) async-start(bf16[64,16,360]{2,1,0:T(8,128)(2,1)} %bitcast.9), calls=%async_computation.1 | async-start | bytes 1572864 | tf_op jit(solution)/shard_map/all_to_all | solution.py:65
  417.6 104.8 %all-gather.1 = bf16[64,45,64]{2,1,0:T(8,128)(2,1)S(1)} all-gather(bf16[1,45,64]{2,1,0:T(8,128)(2,1)S(1)} %bitcast.105), channel_id=1, replica_groups=mesh['section'=2,'expert'=32,'tensor'=8] {'section','expert'}, dimensions={0}, use_global_device_ids=true | all-gather | bytes 374400 | tf_op jit(solution)/shard_map/all_gather | solution.py:87
  522.5 1.1 reshape.326
  523.6 76.3 %all-gather.3 = bf16[64,45,64]{2,1,0:T(8,128)(2,1)S(1)} all-gather(bf16[1,45,64]{2,1,0:T(8,128)(2,1)S(1)} %bitcast.106), channel_id=1, replica_groups=mesh['section'=2,'expert'=32,'tensor'=8] {'section','expert'}, dimensions={0}, use_global_device_ids=true | all-gather | bytes 374400 | tf_op jit(solution)/shard_map/all_gather | solution.py:88
  600.0 1.1 reshape.327
  601.1 0.8 dynamic_slice.3
  601.9 0.8 multiply_cosine_fusion
  602.7 1.1 iota_compare_fusion
  603.8 3.4 reshape.319
  607.2 74.6 %all-gather.13.cloned.1.call-done = bf16[64,45,256]{2,1,0:T(8,128)(2,1)} async-done(((bf16[1,45,256]{2,1,0:T(8,128)(2,1)}), bf16[64,45,256]{2,1,0:T(8,128)(2,1)}) %all-gather.13.cloned.1.call-update) | async-done | bytes 1474576 | tf_op jit(solution)/shard_map/all_gather | solution.py:136
  681.8 2.4 reshape.323
  684.2 2.6 gather_fusion.2
  686.8 1.2 reshape.281
  688.0 0.5 multiply_reduce_fusion
  688.7 18.8 %psum.7 = f32[128]{0:T(128)S(1)} all-reduce(f32[128]{0:T(128)S(1)} %get-tuple-element.8), channel_id=1, replica_groups=mesh['section'=2,'expert'=32,'tensor'=8] {'tensor'}, use_global_device_ids=true, to_apply=%region_7.8 | all-reduce | flops 128 | bytes 1024 | tf_op jit(solution)/shard_map/psum | solution.py:75
  707.8 29.7 %all_gather.29 = bf16[128,2880]{0,1:T(8,128)(2,1)S(1)} all-gather(bf16[128,360]{0,1:T(8,128)(2,1)S(1)} %copy.61), channel_id=1, replica_groups=mesh['section'=2,'expert'=32,'tensor'=8] {'tensor'}, dimensions={1}, use_global_device_ids=true | all-gather | bytes 829440 | tf_op jit(solution)/shard_map/all_gather | solution.py:82
  737.5 1.5 convolution_bitcast_fusion
  739.0 0.7 fusion.38
  739.8 28.8 %all_gather.31 = bf16[4096,64]{0,1:T(8,128)(2,1)S(1)} all-gather(bf16[128,64]{0,1:T(8,128)(2,1)S(1)} %pad_maximum_fusion), channel_id=1, replica_groups=mesh['section'=2,'expert'=32,'tensor'=8] {'expert'}, dimensions={0}, use_global_device_ids=true | all-gather | bytes 540672 | tf_op jit(solution)/shard_map/all_gather | solution.py:108
  768.6 0.7 fusion.48
  769.4 1.3 fusion
  770.7 0.4 convolution_convert_fusion.2
  771.1 30.1 %all_gather.34 = bf16[4096,64]{0,1:T(8,128)(2,1)S(1)} all-gather(bf16[128,64]{0,1:T(8,128)(2,1)S(1)} %convolution_convert_fusion.2), channel_id=1, replica_groups=mesh['section'=2,'expert'=32,'tensor'=8] {'expert'}, dimensions={0}, use_global_device_ids=true | all-gather | bytes 540672 | tf_op jit(solution)/shard_map/all_gather | solution.py:109
  801.2 2.1 fusion.1
  803.2 1.8 fusion.12
  805.1 1.4 convolution_convert_fusion
  806.5 0.8 copy.66
  807.3 39.2 %reduce-scatter.5.cloned.1.call-done = bf16[128,360]{0,1:T(8,128)(2,1)} async-done(((bf16[128,2880]{0,1:T(8,128)(2,1)}), bf16[128,360]{0,1:T(8,128)(2,1)}) %reduce-scatter.5.cloned.1.call-update) | async-done | bytes 92176
  (61 shorter events, 1.9 us)
Async XLA Ops:
  7.2 390.4 %copy-start = (bf16[1,1440,360]{2,1,0:T(8,128)(2,1)S(1)}, bf16[1,1440,360]{2,1,0:T(8,128)(2,1)}, u32[]{:S(2)}) copy-start(bf16[1,1440,360]{2,1,0:T(8,128)(2,1)} %param.16) | copy-start | bytes 3110404
  7.2 1.0 copy-start.1
  8.2 5.7 copy-start.5
  57.0 280.1 %all-to-all-start = ((bf16[64,16,2880]{2,1,0:T(8,128)(2,1)}), bf16[64,16,2880]{2,1,0:T(8,128)(2,1)}, u32[]{:S(2)}, u32[]{:S(2)}) async-start(bf16[64,16,2880]{2,1,0:T(8,128)(2,1)} %broadcast_select_fusion), calls=%async_computation | async-start | bytes 12058624 | tf_op jit(solution)/shard_map/all_to_all | solution.py:51
  75.1 318.2 %all-gather.9.cloned.1.call-start = ((), (), s32[]{:S(2)}) async-start(), calls=%async_computation.3 | async-start | bytes 3391488 | tf_op jit(solution)/shard_map/all_gather | solution.py:62
  344.0 259.9 %all-gather.11.cloned.1.call-start = ((), (), s32[]{:S(2)}) async-start(), calls=%async_computation.4 | async-start | bytes 1597440 | tf_op jit(solution)/shard_map/all_gather | solution.py:86
  344.7 337.1 %all-gather.13.cloned.1.call-start = ((), (), s32[]{:S(2)}) async-start(), calls=%async_computation.5 | async-start | bytes 1597440 | tf_op jit(solution)/shard_map/all_gather | solution.py:136
  400.8 16.7 %copy-start.12 = (f32[128,4]{0,1:T(4,128)S(1)}, f32[128,4]{0,1:T(4,128)}, u32[]{:S(2)}) copy-start(f32[128,4]{0,1:T(4,128)} %param.13) | copy-start | bytes 6148
  400.8 16.8 %copy-start.7 = (bf16[45,64]{1,0:T(8,128)(2,1)S(1)}, bf16[45,64]{1,0:T(8,128)(2,1)}, u32[]{:S(2)}) copy-start(bf16[45,64]{1,0:T(8,128)(2,1)} %param.19) | copy-start | bytes 17284
  400.8 122.8 %copy-start.8 = (bf16[45,64]{1,0:T(8,128)(2,1)S(1)}, bf16[45,64]{1,0:T(8,128)(2,1)}, u32[]{:S(2)}) copy-start(bf16[45,64]{1,0:T(8,128)(2,1)} %param.20) | copy-start | bytes 17284
  402.0 282.2 %all-to-all-start.1 = ((bf16[64,16,360]{2,1,0:T(8,128)(2,1)}), bf16[64,16,360]{2,1,0:T(8,128)(2,1)S(1)}, u32[]{:S(2)}, u32[]{:S(2)}) async-start(bf16[64,16,360]{2,1,0:T(8,128)(2,1)} %bitcast.9), calls=%async_computation.1 | async-start | bytes 1572864 | tf_op jit(solution)/shard_map/all_to_all | solution.py:65
  417.3 429.2 %reduce-scatter.5.cloned.1.call-start = ((), (), s32[]{:S(2)}) async-start(), calls=%async_computation.6 | async-start | bytes 829440
  601.9 5.4 copy-start.9
  601.9 5.3 copy-start.11
  686.8 52.2 %copy-start.10 = (f32[32]{0:T(128)S(1)}, f32[32]{0:T(128)}, u32[]{:S(2)}) copy-start(f32[32]{0:T(128)} %copy-done.9) | copy-start | bytes 388
  688.6 80.8 %copy-start.6 = (f32[128,32]{0,1:T(8,128)S(1)}, f32[128,32]{0,1:T(8,128)}, u32[]{:S(2)}) copy-start(f32[128,32]{0,1:T(8,128)} %get-tuple-element.15) | copy-start | bytes 49156
  688.7 80.7 %copy-start.4 = (pred[128,4096]{0,1:T(8,128)(4,1)S(1)}, pred[128,4096]{0,1:T(8,128)(4,1)}, u32[]{:S(2)}) copy-start(pred[128,4096]{0,1:T(8,128)(4,1)} %iota_compare_fusion) | copy-start | bytes 1572868
  707.8 60.9 %copy-start.2 = (bf16[2880,256]{1,0:T(8,128)(2,1)S(1)}, bf16[2880,256]{1,0:T(8,128)(2,1)}, u32[]{:S(2)}) copy-start(bf16[2880,256]{1,0:T(8,128)(2,1)} %reshape.319) | copy-start | bytes 4423684
  769.4 1.3 copy-start.3
Sparse Core Ops, SparseCore 0:
  344.1 49.0 all-gather.8
  396.5 145.0 all-gather.10
  544.9 136.8 all-gather.12
  806.6 39.8 reduce-scatter.4
where the time goes:
time: 854 us; the launch traced here: 853 us
  waiting for transfers between devices  421 us (49%)
  blocking collectives  319 us (37%)
  local copies, waits for them, and re-layouts  34.3 us (4%)
  starting transfers between devices  33.6 us (4%)
  matrix products  16.1 us (2%)
  other arithmetic  15.2 us (2%)
  between operations  14.2 us (2%)
    all_to_all x1, waiting for transfers between devices, on_device(): lax.all_to_all(outgoing, ('section', 'expert'), split_axis=0, concat_axis...  258 us
    all_gather x1, blocking collectives, on_device(): lax.all_gather(w_key, ('section', 'expert'), axis=0, tiled=True)  105 us
    all_gather x1, blocking collectives, on_device(): lax.all_gather(w_value, ('section', 'expert'), axis=0, tiled=True)  76.3 us
    all_gather x1, waiting for transfers between devices, on_device(): lax.all_gather(w_out, ('section', 'expert'), axis=1, tiled=True)  74.6 us
    all_gather x1, waiting for transfers between devices, on_device(): all_hidden = lax.all_gather(hidden, 'tensor', axis=1, tiled=True)  47.8 us
    unnamed x5, waiting for transfers between devices  40.6 us
    all_gather x1, blocking collectives, on_device(): whole_tokens = lax.all_gather(tokens, 'tensor', axis=1, tiled=True)  30.1 us
    all_gather x1, blocking collectives, on_device(): lax.all_gather(values, 'expert', axis=0, tiled=True)  30.1 us
  transfers between devices with their start and end apart: 6, of which 4 were waited for; matrix products, arithmetic and copies ran while one was open for 3% of the time, Pallas kernels for 0%

commit v1 on v0

--- a/solution.py
+++ b/solution.py
@@ -79,7 +79,15 @@
     normed_part = (
         stream_wide * lax.rsqrt(squares / D + epsilon)[:, None] * gain_part[None, :]
     ).astype(jnp.bfloat16)
-    normed = lax.all_gather(normed_part, "tensor", axis=1, tiled=True)
+    normed = jnp.concatenate(
+        jax.lax.all_to_all(
+            jnp.stack(tuple((normed_part for _ in range(jax.lax.axis_size("tensor"))))),
+            "tensor",
+            0,
+            0,
+        ),
+        axis=1,
+    )
     query_width = w_query.shape[1]
     kv_width = w_key.shape[1]
     pieces = (

time: 854 us -> 802 us (0.939)
  the two profiles are of different devices: /device:TPU:32 before, /device:TPU:4 now
where the time goes in v1:
time: 802 us; the launch traced here: 801 us
  waiting for transfers between devices  396 us (49%)
  blocking collectives  286 us (36%)
  starting transfers between devices  38.4 us (5%)
  local copies, waits for them, and re-layouts  36.5 us (5%)
  matrix products  16 us (2%)
  between operations  14.1 us (2%)
  other arithmetic  14 us (2%)
    all_to_all x1, waiting for transfers between devices, on_device(): lax.all_to_all(outgoing, ('section', 'expert'), split_axis=0, concat_axis...  263 us
    all_gather x1, blocking collectives, on_device(): lax.all_gather(w_key, ('section', 'expert'), axis=0, tiled=True)  105 us
    all_gather x1, blocking collectives, on_device(): lax.all_gather(w_value, ('section', 'expert'), axis=0, tiled=True)  73.9 us
    all_gather x1, waiting for transfers between devices, on_device(): lax.all_gather(w_out, ('section', 'expert'), axis=1, tiled=True)  46.1 us
    unnamed x5, waiting for transfers between devices  44.2 us
    all_gather x1, waiting for transfers between devices, on_device(): all_hidden = lax.all_gather(hidden, 'tensor', axis=1, tiled=True)  43 us
    all_gather x1, blocking collectives, on_device(): lax.all_gather(keys, 'expert', axis=0, tiled=True)  30.3 us
    all_gather x1, blocking collectives, on_device(): whole_tokens = lax.all_gather(tokens, 'tensor', axis=1, tiled=True)  29.8 us
  transfers between devices with their start and end apart: 7, of which 4 were waited for; matrix products, arithmetic and copies ran while one was open for 4% of the time, Pallas kernels for 0%

profile of v1, /device:TPU:4, one launch (start us, length us, event | category | flops | bytes accessed | tf_op | source)
XLA Modules:
  0.0 801.3 jit_solution(10435351109936303661)
XLA Ops:
  7.2 0.8 compare_select_fusion.2
  8.2 3.3 gather_fusion
  11.6 1.2 reduce-window.6
  13.2 0.4 fusion.7
  13.6 0.3 select_reduce_fusion
  13.9 29.8 %all_gather.24 = bf16[128,2880]{0,1:T(8,128)(2,1)S(1)} all-gather(bf16[128,360]{0,1:T(8,128)(2,1)S(1)} %copy-done.5), channel_id=1, replica_groups=mesh['section'=2,'expert'=32,'tensor'=8] {'tensor'}, dimensions={1}, use_global_device_ids=true | all-gather | bytes 829440 | tf_op jit(solution)/shard_map/all_gather | solution.py:47
  43.7 0.4 copy.44
  44.2 6.6 gather_fusion.1
  50.8 5.9 broadcast_select_fusion
  56.7 18.9 %all-to-all-start = ((bf16[64,16,2880]{2,1,0:T(8,128)(2,1)}), bf16[64,16,2880]{2,1,0:T(8,128)(2,1)}, u32[]{:S(2)}, u32[]{:S(2)}) async-start(bf16[64,16,2880]{2,1,0:T(8,128)(2,1)} %broadcast_select_fusion), calls=%async_computation | async-start | bytes 12058624 | tf_op jit(solution)/shard_map/all_to_all | solution.py:51
  75.6 1.8 copy.45
  77.4 2.3 reshape_squeeze.3
  79.8 262.8 %all-to-all-done = bf16[64,16,2880]{2,1,0:T(8,128)(2,1)} async-done(((bf16[64,16,2880]{2,1,0:T(8,128)(2,1)}), bf16[64,16,2880]{2,1,0:T(8,128)(2,1)}, u32[]{:S(2)}, u32[]{:S(2)}) %all-to-all-start) | async-done | bytes 5898272 | tf_op jit(solution)/shard_map/all_to_all | solution.py:51
  342.6 5.8 fusion.47
  348.4 1.0 fusion.19
  349.5 0.7 all-gather.11.cloned.1.call-update
  350.2 43.0 %all-gather.9.cloned.1.call-done = bf16[8,180,1024]{2,1,0:T(8,128)(2,1)} async-done(((bf16[1,180,1024]{2,1,0:T(8,128)(2,1)}), bf16[8,180,1024]{2,1,0:T(8,128)(2,1)}) %all-gather.9.cloned.1.call-update) | async-done | bytes 2949136 | tf_op jit(solution)/shard_map/all_gather | solution.py:62
  393.2 4.3 reshape.323
  397.6 3.2 convolution_convert_fusion.1
  400.8 1.2 copy.46
  402.0 15.8 %all-to-all-start.1 = ((bf16[64,16,360]{2,1,0:T(8,128)(2,1)}), bf16[64,16,360]{2,1,0:T(8,128)(2,1)S(1)}, u32[]{:S(2)}, u32[]{:S(2)}) async-start(bf16[64,16,360]{2,1,0:T(8,128)(2,1)} %bitcast.9), calls=%async_computation.1 | async-start | bytes 1572864 | tf_op jit(solution)/shard_map/all_to_all | solution.py:65
  417.9 0.7 all-gather.13.cloned.1.call-update
  418.6 105.3 %all-gather.1 = bf16[64,45,64]{2,1,0:T(8,128)(2,1)S(1)} all-gather(bf16[1,45,64]{2,1,0:T(8,128)(2,1)S(1)} %bitcast.115), channel_id=1, replica_groups=mesh['section'=2,'expert'=32,'tensor'=8] {'section','expert'}, dimensions={0}, use_global_device_ids=true | all-gather | bytes 374400 | tf_op jit(solution)/shard_map/all_gather | solution.py:95
  524.1 1.1 reshape.335
  525.3 73.9 %all-gather.3 = bf16[64,45,64]{2,1,0:T(8,128)(2,1)S(1)} all-gather(bf16[1,45,64]{2,1,0:T(8,128)(2,1)S(1)} %bitcast.116), channel_id=1, replica_groups=mesh['section'=2,'expert'=32,'tensor'=8] {'section','expert'}, dimensions={0}, use_global_device_ids=true | all-gather | bytes 374400 | tf_op jit(solution)/shard_map/all_gather | solution.py:96
  599.2 1.1 reshape.336
  600.3 0.8 dynamic_slice.3
  601.3 1.9 gather_fusion.2
  603.5 0.5 multiply_reduce_fusion
  604.1 18.2 %psum.7 = f32[128]{0:T(128)S(1)} all-reduce(f32[128]{0:T(128)S(1)} %get-tuple-element.6), channel_id=1, replica_groups=mesh['section'=2,'expert'=32,'tensor'=8] {'tensor'}, use_global_device_ids=true, to_apply=%region_7.8 | all-reduce | flops 128 | bytes 1024 | tf_op jit(solution)/shard_map/psum | solution.py:75
  622.6 1.0 stack.2
  623.6 3.5 all-to-all-start.2
  627.2 1.1 iota_compare_fusion
  628.3 3.4 reshape.327
  631.7 1.8 copy.50
  633.6 46.1 %all-gather.13.cloned.1.call-done = bf16[64,45,256]{2,1,0:T(8,128)(2,1)} async-done(((bf16[1,45,256]{2,1,0:T(8,128)(2,1)}), bf16[64,45,256]{2,1,0:T(8,128)(2,1)}) %all-gather.13.cloned.1.call-update) | async-done | bytes 1474576 | tf_op jit(solution)/shard_map/all_gather | solution.py:144
  679.7 3.4 reshape.331
  683.1 1.5 convolution_bitcast_fusion
  684.8 30.3 %all_gather.27 = bf16[4096,64]{0,1:T(8,128)(2,1)S(1)} all-gather(bf16[128,64]{0,1:T(8,128)(2,1)S(1)} %pad_maximum_fusion), channel_id=1, replica_groups=mesh['section'=2,'expert'=32,'tensor'=8] {'expert'}, dimensions={0}, use_global_device_ids=true | all-gather | bytes 540672 | tf_op jit(solution)/shard_map/all_gather | solution.py:116
  715.1 0.6 fusion.48
  715.7 1.3 fusion
  717.0 0.4 convolution_convert_fusion.2
  717.4 28.5 %all_gather.30 = bf16[4096,64]{0,1:T(8,128)(2,1)S(1)} all-gather(bf16[128,64]{0,1:T(8,128)(2,1)S(1)} %convolution_convert_fusion.2), channel_id=1, replica_groups=mesh['section'=2,'expert'=32,'tensor'=8] {'expert'}, dimensions={0}, use_global_device_ids=true | all-gather | bytes 540672 | tf_op jit(solution)/shard_map/all_gather | solution.py:117
  745.9 2.1 fusion.1
  748.0 1.8 fusion.12
  749.8 1.4 convolution_convert_fusion
  751.3 0.8 copy.53
  752.0 42.8 %reduce-scatter.5.cloned.1.call-done = bf16[128,360]{0,1:T(8,128)(2,1)} async-done(((bf16[128,2880]{0,1:T(8,128)(2,1)}), bf16[128,360]{0,1:T(8,128)(2,1)}) %reduce-scatter.5.cloned.1.call-update) | async-done | bytes 92176
  (56 shorter events, 2.1 us)
Async XLA Ops:
  7.2 390.4 %copy-start = (bf16[1,1440,360]{2,1,0:T(8,128)(2,1)S(1)}, bf16[1,1440,360]{2,1,0:T(8,128)(2,1)}, u32[]{:S(2)}) copy-start(bf16[1,1440,360]{2,1,0:T(8,128)(2,1)} %param.16) | copy-start | bytes 3110404
  7.2 1.0 copy-start.1
  8.2 5.7 copy-start.5
  56.7 285.9 %all-to-all-start = ((bf16[64,16,2880]{2,1,0:T(8,128)(2,1)}), bf16[64,16,2880]{2,1,0:T(8,128)(2,1)}, u32[]{:S(2)}, u32[]{:S(2)}) async-start(bf16[64,16,2880]{2,1,0:T(8,128)(2,1)} %broadcast_select_fusion), calls=%async_computation | async-start | bytes 12058624 | tf_op jit(solution)/shard_map/all_to_all | solution.py:51
  75.6 317.7 %all-gather.9.cloned.1.call-start = ((), (), s32[]{:S(2)}) async-start(), calls=%async_computation.4 | async-start | bytes 3391488 | tf_op jit(solution)/shard_map/all_gather | solution.py:62
  349.5 278.9 %all-gather.11.cloned.1.call-start = ((), (), s32[]{:S(2)}) async-start(), calls=%async_computation.5 | async-start | bytes 1597440 | tf_op jit(solution)/shard_map/all_gather | solution.py:94
  400.8 17.8 %copy-start.6 = (bf16[45,64]{1,0:T(8,128)(2,1)S(1)}, bf16[45,64]{1,0:T(8,128)(2,1)}, u32[]{:S(2)}) copy-start(bf16[45,64]{1,0:T(8,128)(2,1)} %param.19) | copy-start | bytes 17284
  400.8 123.2 %copy-start.8 = (f32[128,4]{0,1:T(4,128)S(1)}, f32[128,4]{0,1:T(4,128)}, u32[]{:S(2)}) copy-start(f32[128,4]{0,1:T(4,128)} %param.13) | copy-start | bytes 6148
  400.8 124.4 %copy-start.7 = (bf16[45,64]{1,0:T(8,128)(2,1)S(1)}, bf16[45,64]{1,0:T(8,128)(2,1)}, u32[]{:S(2)}) copy-start(bf16[45,64]{1,0:T(8,128)(2,1)} %param.20) | copy-start | bytes 17284
  402.0 199.3 %all-to-all-start.1 = ((bf16[64,16,360]{2,1,0:T(8,128)(2,1)}), bf16[64,16,360]{2,1,0:T(8,128)(2,1)S(1)}, u32[]{:S(2)}, u32[]{:S(2)}) async-start(bf16[64,16,360]{2,1,0:T(8,128)(2,1)} %bitcast.9), calls=%async_computation.1 | async-start | bytes 1572864 | tf_op jit(solution)/shard_map/all_to_all | solution.py:65
  417.8 261.9 %all-gather.13.cloned.1.call-start = ((), (), s32[]{:S(2)}) async-start(), calls=%async_computation.6 | async-start | bytes 1597440 | tf_op jit(solution)/shard_map/all_gather | solution.py:144
  623.6 59.5 %all-to-all-start.2 = ((bf16[8,128,360]{1,2,0:T(8,128)(2,1)}), bf16[8,128,360]{1,2,0:T(8,128)(2,1)S(1)}, u32[]{:S(2)}, u32[]{:S(2)}) async-start(bf16[8,128,360]{1,2,0:T(8,128)(2,1)} %stack.2), calls=%async_computation.2 | async-start | bytes 1474560 | tf_op jit(solution)/shard_map/all_to_all | solution.py:83
  627.1 167.7 %reduce-scatter.5.cloned.1.call-start = ((), (), s32[]{:S(2)}) async-start(), calls=%async_computation.7 | async-start | bytes 829440
  683.1 32.6 %copy-start.4 = (pred[128,4096]{0,1:T(8,128)(4,1)S(1)}, pred[128,4096]{0,1:T(8,128)(4,1)}, u32[]{:S(2)}) copy-start(pred[128,4096]{0,1:T(8,128)(4,1)} %iota_compare_fusion) | copy-start | bytes 1572868
  715.7 1.3 copy-start.3
  748.0 1.8 copy-start.2
Sparse Core Ops, SparseCore 0:
  349.6 43.6 all-gather.8
  396.5 142.8 all-gather.10
  542.8 136.8 all-gather.12
  751.4 43.3 reduce-scatter.4
